TPU v7x, 256 devices: a whole 4x4x8 slice. The times are simulated.
256 devices in a mesh: tm: 16 (over x, y_lo, core), batch: 16 (over z, y_hi).
Axes of the slice: x: 4, y: 4 (y_hi: 2, y_lo: 2; y = y_hi * 2 + y_lo), z: 8, core: 2. Of those that a mesh axis runs over, the one named last changes fastest.
Arguments:
- signal: bfloat16 [16, 2048, 4096], P('batch', 'tm'), may hold values from -7.5 to 7.5
- gate_input: bfloat16 [16, 2048, 4096], P('batch', 'tm'), may hold values from -6 to 6
- bc_forward: bfloat16 [16, 2048, 128], P('batch', 'tm'), may hold values from -6 to 6
- bc_backward: bfloat16 [16, 2048, 128], P('batch', 'tm'), may hold values from -6 to 6
- step_raw: bfloat16 [16, 2048, 128], P('batch', 'tm'), may hold values from -12 to 2
- decay_rate: float32 [2, 64], replicated, may hold values from 0.3 to 1
- conv_weight: float32 [2, 4, 4224], replicated, may hold values from -3 to 3
- conv_bias: float32 [2, 4224], replicated, may hold values from -1.5 to 1.5
- skip_gain: float32 [2, 64], replicated, may hold values from 0.5 to 1.5
- norm_gain: float32 [4096], replicated, may hold values from 0.1 to 1.9
Outputs:
- mixed: bfloat16 [16, 2048, 4096], P(None, 'batch', 'tm')
All inputs are finite; a program needn't handle non-finite values.
Results may differ from a plain program's by a relative error of at most 0.0075.
Values may be sent and summed in bfloat16 or wider, within the bound.
No kernel may reach another device: no remote copies, remote signals or barrier semaphores. Data moves between devices by JAX's collectives and lax.ppermute only.
A program may use at most 256 MiB of HBM per device.

v0:
```python
import jax
import jax.numpy as jnp
from jax import lax
from jax.sharding import PartitionSpec as P

INNER = 4096
HEADDIM = 64
STATE = 64
GROUP = 128
HEADS = 64


EPSILON = 1e-05


def from_behind(array, axis, by):
    devices = lax.axis_size(axis)
    pairs = [(i, i + by) for i in range(devices) if 0 <= i + by < devices]
    return lax.ppermute(array, axis, pairs)


def entering(value, axis, join, neutral):
    count, mine = (lax.axis_size(axis), lax.axis_index(axis))
    pieces = jax.tree.map(lambda part: lax.all_gather(part, axis), value)
    running = jax.tree.map(
        lambda part, zero: jnp.full_like(part, 0) + jnp.asarray(zero, part.dtype), value, neutral
    )

    def lap(position, running):
        longer = join(running, jax.tree.map(lambda part: part[position], pieces))
        return jax.tree.map(lambda new, old: jnp.where(position < mine, new, old), longer, running)

    return lax.fori_loop(0, count - 1, lap, running)


def carried_in(array, axis, join, neutral):
    count = lax.axis_size(axis)
    place = lax.axis_index(axis)
    ahead = count - 1 - place
    gathered = jax.tree.map(
        lambda a, kind: lax.all_gather(a.astype(kind), axis), array, (jnp.bfloat16, jnp.bfloat16)
    )
    state = jax.tree.map(lambda a, e: jnp.zeros_like(a) + jnp.asarray(e, a.dtype), array, neutral)

    def one(lap, state):
        source = count - 1 - lap
        return join(
            state,
            jax.tree.map(
                lambda a, own: lax.dynamic_index_in_dim(a, source, 0, False).astype(own.dtype),
                gathered,
                array,
            ),
        )

    return lax.fori_loop(0, ahead, one, state)


def conv_silu(sequence, history, weights, offsets):
    length = sequence.shape[0]
    padded = jnp.concatenate([history, sequence], 0).astype(jnp.float32)
    combined_waveform = jnp.broadcast_to(offsets[None, :], (length, sequence.shape[1]))
    for offset in range(weights.shape[0]):
        combined_waveform = (
            combined_waveform + weights[offset][None, :] * padded[offset : offset + length]
        )
    return jax.nn.silu(combined_waveform).astype(jnp.bfloat16)


def block_parts(x_part, b_part, step_size, rate_head):
    log_decay = -step_size * rate_head[None, None, :]
    cum_log = jnp.cumsum(log_decay, axis=1)
    weight_end = jnp.exp(cum_log[:, -1:, :] - cum_log) * step_size
    b_scaled = (b_part.astype(jnp.float32)[:, :, None, :] * weight_end[..., None]).astype(
        jnp.bfloat16
    )
    states = jnp.einsum("mqhn,mqhp->mhnp", b_scaled, x_part, preferred_element_type=jnp.float32)
    return (cum_log, states, jnp.exp(cum_log[:, -1, :]))


def prepare(x_conv, bc_conv, step_raw, rate_head):
    block_count = x_conv.shape[0] // GROUP
    x_part = x_conv.reshape(block_count, GROUP, -1, HEADDIM)
    b_part = bc_conv[:, :STATE].reshape(block_count, GROUP, STATE)
    c_part = bc_conv[:, STATE:].reshape(block_count, GROUP, STATE)
    step_size = jax.nn.softplus(step_raw.astype(jnp.float32)).reshape(block_count, GROUP, -1)
    cum_log, states, decays = block_parts(x_part, b_part, step_size, rate_head)
    return (x_part, b_part, c_part, step_size, cum_log, states, decays)


def summarize(states, decays):

    def absorb(state_in, pieces):
        return (pieces[1][:, None, None] * state_in + pieces[0], None)

    final_state, _ = lax.scan(absorb, jnp.zeros(states.shape[1:], jnp.float32), (states, decays))
    return (jnp.prod(decays, axis=0), final_state)


def carried_term(c_block, state_in):
    state_high = state_in.astype(jnp.bfloat16)
    state_low = (state_in - state_high.astype(jnp.float32)).astype(jnp.bfloat16)
    upper = jnp.einsum("in,hnp->ihp", c_block, state_high, preferred_element_type=jnp.float32)
    lower = jnp.einsum("in,hnp->ihp", c_block, state_low, preferred_element_type=jnp.float32)
    return upper + lower


def block_outputs(parts, start, skip_head):
    block_len = parts[0].shape[1]
    causal_mask = jnp.arange(block_len)[:, None] >= jnp.arange(block_len)[None, :]

    def advance(state_in, pieces):
        x_block, b_block, c_block, step_block, cum_block, state_block, decay_block = pieces
        scores = jnp.dot(c_block, b_block.T, preferred_element_type=jnp.float32)
        differ = cum_block.T[:, :, None] - cum_block.T[:, None, :]
        masked = jnp.where(causal_mask[None], jnp.exp(jnp.minimum(differ, 0.0)), 0.0)
        mixing = (masked * scores[None] * step_block.T[:, None, :]).astype(jnp.bfloat16)
        local_out = jnp.einsum("hij,jhp->ihp", mixing, x_block, preferred_element_type=jnp.float32)
        carried = carried_term(c_block, state_in)
        result = (
            local_out
            + jnp.exp(cum_block)[:, :, None] * carried
            + skip_head[None, :, None] * x_block.astype(jnp.float32)
        )
        new_state = decay_block[:, None, None] * state_in + state_block
        return (new_state, result.astype(jnp.bfloat16))

    _, outputs = lax.scan(advance, start, parts)
    return outputs.reshape(outputs.shape[0] * outputs.shape[1], -1)


def combine(earlier, later):
    return (earlier[0] * later[0], earlier[1] * later[0][:, None, None] + later[1])


def gated_rows(forward_out, backward_out, gate_rows):
    return (forward_out.astype(jnp.float32) + backward_out.astype(jnp.float32)) * jax.nn.silu(
        gate_rows.astype(jnp.float32)
    )


def shards(
    signal,
    gate_input,
    bc_forward,
    bc_backward,
    step_raw,
    decay_rate,
    conv_weight,
    conv_bias,
    skip_gain,
    norm_gain,
):
    rim_rows = conv_weight.shape[1] - 1
    signal_dev = signal[0]
    bcf_dev = bc_forward[0]
    bcb_dev = bc_backward[0]
    step_dev = step_raw[0]
    left_rim = from_behind(
        jnp.concatenate([signal_dev[-rim_rows:], bcf_dev[-rim_rows:]], 1), "tm", 1
    )
    right_rim = from_behind(
        jnp.concatenate([signal_dev[:rim_rows], bcb_dev[:rim_rows]], 1), "tm", -1
    )
    fwd_parts = prepare(
        conv_silu(signal_dev, left_rim[:, :INNER], conv_weight[0, :, :INNER], conv_bias[0, :INNER]),
        conv_silu(bcf_dev, left_rim[:, INNER:], conv_weight[0, :, INNER:], conv_bias[0, INNER:]),
        step_dev[:, :HEADS],
        decay_rate[0],
    )
    back_history = right_rim[::-1]
    bwd_parts = prepare(
        conv_silu(
            signal_dev[::-1],
            back_history[:, :INNER],
            conv_weight[1, :, :INNER],
            conv_bias[1, :INNER],
        ),
        conv_silu(
            bcb_dev[::-1], back_history[:, INNER:], conv_weight[1, :, INNER:], conv_bias[1, INNER:]
        ),
        step_dev[::-1, HEADS:],
        decay_rate[1],
    )
    fwd_decay, fwd_state = summarize(fwd_parts[5], fwd_parts[6])
    bwd_decay, bwd_state = summarize(bwd_parts[5], bwd_parts[6])
    empty_decay = jnp.ones((HEADS,), jnp.float32)
    empty_state = jnp.zeros((HEADS, STATE, HEADDIM), jnp.float32)
    fwd_in = entering((fwd_decay, fwd_state), "tm", combine, (empty_decay, empty_state))
    bwd_in = carried_in((bwd_decay, bwd_state), "tm", combine, (empty_decay, empty_state))
    forward_out = block_outputs(fwd_parts, fwd_in[1], skip_gain[0])
    backward_out = block_outputs(bwd_parts, bwd_in[1], skip_gain[1])[::-1]
    gated = gated_rows(forward_out, backward_out, gate_input[0])
    inv_rms = lax.rsqrt(jnp.mean(gated * gated, axis=-1, keepdims=True) + EPSILON)
    normed = (gated * inv_rms * norm_gain[None, :]).astype(jnp.bfloat16)
    return lax.all_to_all(
        lax.all_to_all(normed[None], "tm", split_axis=2, concat_axis=1, tiled=True),
        "batch",
        split_axis=1,
        concat_axis=0,
        tiled=True,
    )


def solution(mesh):
    in_specs = (
        P("batch", "tm", None),
        P("batch", "tm", None),
        P("batch", "tm", None),
        P("batch", "tm", None),
        P("batch", "tm", None),
        P(),
        P(),
        P(),
        P(),
        P(),
    )
    out_specs = P(None, "batch", "tm")
    return jax.shard_map(shards, mesh=mesh, in_specs=in_specs, out_specs=out_specs, check_vma=False)
```

profile of v0, /device:TPU:2, one launch (start us, length us, event | category | flops | bytes accessed | tf_op | source)
XLA Modules:
  0.0 469.8 jit_solution(14375612540284527570)
XLA Ops:
  8.2 1.9 collective-permute-start
  10.9 4.5 collective-permute-start.1
  15.4 1.9 fusion.75
  35.5 2.4 add_convert_fusion
  40.8 2.0 convolution_add_fusion
  43.7 16.9 %all-gather.2 = bf16[16,1,64]{2,1,0:T(2,128)(2,1)S(1)} all-gather(bf16[1,1,64]{2,1,0:T(2,128)(2,1)S(1)} %copy-done.21), channel_id=4, replica_groups=mesh['tm'=16,'batch'=16] {'tm'}, dimensions={0}, use_global_device_ids=true | all-gather | bytes 2176 | tf_op jit(solution)/shard_map/all_gather | solution.py:41
  61.4 16.3 %all-gather = f32[16,1,64]{2,1,0:T(1,128)S(1)} all-gather(f32[1,1,64]{2,1,0:T(1,128)S(1)} %get-tuple-element.350), channel_id=2, replica_groups=mesh['tm'=16,'batch'=16] {'tm'}, dimensions={0}, use_global_device_ids=true | all-gather | bytes 4352 | tf_op jit(solution)/shard_map/all_gather | solution.py:24
  78.1 56.9 %all-gather.9.cloned.1.call-done = bf16[1024,64,64]{2,1,0:T(8,128)(2,1)} async-done(((bf16[64,64,64]{2,1,0:T(8,128)(2,1)}), bf16[1024,64,64]{2,1,0:T(8,128)(2,1)}) %all-gather.9.cloned.1.call-update) | async-done | bytes 8388624 | tf_op jit(solution)/shard_map/all_gather | solution.py:41
  135.2 19.8 %while.18 = (s32[]{:T(128)}, f32[64,64,64]{2,1,0:T(8,128)S(1)}, s32[]{:T(128)}, bf16[16,64]{1,0:T(8,128)(2,1)S(1)}, bf16[16,64,64,64]{3,2,1,0:T(8,128)(2,1)}, /*index=5*/s32[]{:T(128)}, s32[]{:T(128)}, s32[]{:T(128)}, s32[]{:T(128)}) while((s32[]{:T(128)}, f32[64,64,64]{2,1,0:T(8,128)S(1)}, s32[]{:T(128)}, bf16[16,64]{1,0:T(8,128)(2,1)S(1)}, ...), condition=%wide.region_5.6_spmd, body=%wide.region_4.5_spmd.sunk | while | flops 786502 | bytes 2622235 | solution.py:56
  135.2 1.7 convert_add_fusion.2
  137.0 1.7 convert_add_fusion.2
  138.7 1.7 convert_add_fusion.2
  140.5 1.7 convert_add_fusion.2
  142.2 1.7 convert_add_fusion.2
  144.0 1.7 convert_add_fusion.2
  145.7 1.7 convert_add_fusion.2
  149.2 2.0 convert_add_fusion.2
  151.3 1.8 convert_add_fusion.2
  160.5 2.5 fusion.16
  164.3 12.6 %rev.16 = bf16[128,4096]{1,0:T(8,128)(2,1)S(1)} reverse(bf16[128,4096]{1,0:T(8,128)(2,1)} %copy.108), dimensions={0} | reverse | bytes 2097152 | tf_op jit(solution)/shard_map/rev | solution.py:192
  176.9 133.6 %all-gather.7.cloned.1.call-done = f32[1024,64,64]{2,1,0:T(8,128)} async-done(((f32[64,64,64]{2,1,0:T(8,128)}), f32[1024,64,64]{2,1,0:T(8,128)}) %all-gather.7.cloned.1.call-update) | async-done | bytes 16777232 | tf_op jit(solution)/shard_map/all_gather | solution.py:24
  310.6 31.9 %while.19 = (s32[]{:T(128)}, f32[64,64,64]{2,1,0:T(8,128)S(1)}, s32[]{:T(128)}, f32[16,64]{1,0:T(8,128)S(1)}, f32[16,64,64,64]{3,2,1,0:T(8,128)}, /*index=5*/s32[]{:T(128)}, s32[]{:T(128)}) while((s32[]{:T(128)}, f32[64,64,64]{2,1,0:T(8,128)S(1)}, s32[]{:T(128)}, f32[16,64]{1,0:T(8,128)S(1)}, f32[16,64,64,64]{3,2,1,0:T(8,128)}, ...), condition=%wide.region_2.3_spmd.clone, body=%wide.region_1.2_spmd.clone.sunk | while | flops 1048580 | bytes 3146609 | solution.py:33
  310.6 2.1 fusion.86
  312.7 2.1 fusion.86
  314.8 2.1 fusion.86
  316.9 2.1 fusion.86
  319.1 2.1 fusion.86
  321.2 2.1 fusion.86
  323.3 2.1 fusion.86
  325.5 2.1 fusion.86
  327.6 2.1 fusion.86
  329.7 2.1 fusion.86
  331.8 2.1 fusion.86
  334.0 2.1 fusion.86
  336.1 2.1 fusion.86
  338.2 2.1 fusion.86
  340.3 2.1 fusion.86
  342.4 1.9 subtract_convert_fusion.1
  346.0 1.8 fusion.67
  350.3 2.5 fusion.18
  354.4 1.9 copy.109
  356.3 2.1 multiply_reduce_fusion
  358.7 2.8 copy.110
  362.1 22.4 %reduce = bf16[4096,128]{1,0:T(8,128)(2,1)S(1)} reduce(bf16[4096,1,128]{2,1,0:T(2,128)(2,1)S(1)} %bitcast.171, bf16[]{:T(256)} %broadcast.103), dimensions={1}, to_apply=%bitcast.145.reduce_sub_computation | reduce | bytes 2097154
  384.8 19.7 %all_to_all.30 = bf16[16,2,16384]{2,1,0:T(2,128)(2,1)S(1)} all-to-all(bf16[16,2,16384]{2,1,0:T(2,128)(2,1)S(1)} %reshape.251), channel_id=1, replica_groups=mesh['tm'=16,'batch'=16] {'tm'}, dimensions={0} | all-to-all | bytes 2097152 | tf_op jit(solution)/shard_map/all_to_all | solution.py:197
  407.0 3.2 copy.119
  410.2 10.6 %reduce.1 = bf16[2048,256]{1,0:T(8,128)(2,1)S(1)} reduce(bf16[2048,1,256]{2,1,0:T(2,128)(2,1)S(1)} %bitcast.172, bf16[]{:T(256)} %broadcast.103), dimensions={1}, to_apply=%bitcast.160.reduce_sub_computation | reduce | bytes 2097154
  421.1 39.7 %all_to_all.31 = bf16[16,2,16384]{2,1,0:T(2,128)(2,1)S(1)} all-to-all(bf16[16,2,16384]{2,1,0:T(2,128)(2,1)S(1)} %reshape.253), channel_id=1, replica_groups=mesh['tm'=16,'batch'=16] {'batch'}, dimensions={0} | all-to-all | bytes 2097152 | tf_op jit(solution)/shard_map/all_to_all | solution.py:196
  (156 shorter events, 47.7 us)
Async XLA Ops:
  6.5 20.7 %copy-start.1 = (bf16[1,128,4096]{2,1,0:T(8,128)(2,1)S(1)}, bf16[1,128,4096]{2,1,0:T(8,128)(2,1)}, u32[]{:S(2)}) copy-start(bf16[1,128,4096]{2,1,0:T(8,128)(2,1)} %param.14) | copy-start | bytes 3145732
  6.5 128.4 %all-gather.9.cloned.1.call-start = ((), (), s32[]{:S(2)}) async-start(), calls=%async_computation.3 | async-start | bytes 17825792 | tf_op jit(solution)/shard_map/all_gather | solution.py:41
  8.2 21.8 %collective-permute-start = (bf16[3,4224]{1,0:T(4,128)(2,1)S(1)}, bf16[3,4224]{1,0:T(4,128)(2,1)S(1)}, u32[]{:S(2)}, u32[]{:S(2)}) collective-permute-start(bf16[3,4224]{1,0:T(4,128)(2,1)S(1)} %pad_maximum_fusion), channel_id=1, source_target_pairs={{0,16},{16,32},{32,48},{48,64},{64,80},{80,96},{96,112},{112,128},... | collective-permute-start | bytes 76040 | tf_op jit(solution)/shard_map/ppermute | solution.py:19
  10.9 18.3 %collective-permute-start.1 = (bf16[3,4224]{1,0:T(4,128)(2,1)S(1)}, bf16[3,4224]{1,0:T(4,128)(2,1)S(1)}, u32[]{:S(2)}, u32[]{:S(2)}) collective-permute-start(bf16[3,4224]{1,0:T(4,128)(2,1)S(1)} %pad_maximum_fusion.1), channel_id=1, source_target_pairs={{16,0},{32,16},{48,32},{64,48},{80,64},{96,80},{112,96},{128,112},... | collective-permute-start | bytes 76040 | tf_op jit(solution)/shard_map/ppermute | solution.py:19
  30.1 1.9 copy-start.15
  33.3 0.8 copy-start.9
  33.3 0.8 copy-start.10
  34.1 3.9 copy-start.6
  34.3 3.9 copy-start.8
  35.4 2.9 copy-start.16
  37.9 0.8 copy-start.11
  37.9 0.8 copy-start.12
  37.9 0.8 copy-start.13
  38.0 0.8 copy-start.14
  38.0 272.6 %all-gather.7.cloned.1.call-start = ((), (), s32[]{:S(2)}) async-start(), calls=%async_computation.2 | async-start | bytes 35651584 | tf_op jit(solution)/shard_map/all_gather | solution.py:24
  40.7 2.0 copy-start.2
  40.8 2.9 copy-start.21
  42.8 35.0 %copy-start.20 = (f32[2,64]{1,0:T(2,128)S(1)}, f32[2,64]{1,0:T(2,128)}, u32[]{:S(2)}) copy-start(f32[2,64]{1,0:T(2,128)} %param.22) | copy-start | bytes 1540
  159.3 1.3 copy-start.7
  159.3 1.2 copy-start.18
  163.0 147.6 %copy-start = (f32[64,64,64]{2,1,0:T(8,128)S(1)}, f32[64,64,64]{2,1,0:T(8,128)}, u32[]{:S(2)}) copy-start(f32[64,64,64]{2,1,0:T(8,128)} %custom-call) | copy-start | bytes 3145732
  345.9 1.8 copy-start.4
  347.7 1.1 copy-start.17
  348.4 1.2 copy-start.3
  348.4 1.9 copy-start.5
  356.3 2.1 copy-start.19
Sparse Core Ops, SparseCore 0:
  38.0 96.8 all-gather.8
  136.8 173.7 all-gather.6
where the time goes:
time: 474 us; the launch traced here: 470 us
  waiting for transfers between devices  191 us (40%)
  other arithmetic  97.9 us (21%)
  blocking collectives  92.6 us (20%)
  local copies, waits for them, and re-layouts  54.4 us (11%)
  between operations  14 us (3%)
  matrix products  12.7 us (3%)
  starting transfers between devices  6.51 us (1%)
    all_gather x1, waiting for transfers between devices, entering(): pieces = jax.tree.map(lambda part: lax.all_gather(part, axis), value)  134 us
    all_gather x1, waiting for transfers between devices, carried_in(): lax.all_gather(a.astype(kind), axis)  56.9 us
    all_to_all x1, blocking collectives, shards(): lax.all_to_all(lax.all_to_all(normed[None], 'tm', split_axis=2, concat_ax...  39.7 us
    unnamed x3, other arithmetic  33 us
    select_n x15, other arithmetic, lap(): jnp.where(position < mine, new, old)  31.2 us
    all_to_all x1, blocking collectives, shards(): lax.all_to_all(normed[None], 'tm', split_axis=2, concat_axis=1, tiled=True)  19.7 us
    add x11, other arithmetic, combine(): earlier[1] * later[0][:, None, None] + later[1]  19.2 us
    all_gather x1, blocking collectives, carried_in(): lax.all_gather(a.astype(kind), axis)  16.9 us
  transfers between devices with their start and end apart: 4, of which 2 were waited for; matrix products, arithmetic and copies ran while one was open for 13% of the time, Pallas kernels for 0%

commit v1 on v0

v1 whole, which is shorter than its diff:
```python
import functools

import jax
import jax.numpy as jnp
from jax import lax
from jax.experimental import pallas as pl
from jax.experimental.pallas import tpu as pltpu
from jax.sharding import PartitionSpec as P

INNER = 4096
HEADDIM = 64
STATE = 64
GROUP = 128
HEADS = 64
BLOCKS = 16
OWN = 4
WIDE = OWN * HEADDIM
ROWS = 2 * GROUP + 8
EPSILON = 1e-05
LOG2E = 1.4426950408889634
VMEM = pl.BlockSpec(memory_space=pltpu.VMEM)
SMEM = pl.BlockSpec(memory_space=pltpu.SMEM)


def pack_kernel(signal, bcf, bcb, step, out):
    both = jnp.concatenate([bcf[0], bcb[0]], axis=1)
    steps = step[0].astype(jnp.float32).T
    for c in range(BLOCKS):
        out[c, :GROUP] = signal[0, :, c * WIDE : (c + 1) * WIDE]
        out[c, GROUP : 2 * GROUP] = both
        mine = jnp.concatenate(
            [steps[c * OWN : (c + 1) * OWN], steps[HEADS + c * OWN : HEADS + (c + 1) * OWN]], axis=0
        )
        out[c, 2 * GROUP :] = jnp.concatenate([mine, jnp.zeros_like(mine)], axis=1).astype(
            jnp.bfloat16
        )


def spread(column, base):
    low = lax.broadcasted_iota(jnp.int32, (GROUP, 128), 1) < HEADDIM
    parts = []
    for p in range(OWN // 2):
        first = column[:, base + 2 * p : base + 2 * p + 1]
        second = column[:, base + 2 * p + 1 : base + 2 * p + 2]
        parts.append(jnp.where(low, first, second))
    return jnp.concatenate(parts, axis=1)


def spread_row(rows, base):
    low = lax.broadcasted_iota(jnp.int32, (1, 128), 1) < HEADDIM
    parts = []
    for p in range(OWN // 2):
        parts.append(
            jnp.where(low, rows[base + 2 * p : base + 2 * p + 1], rows[base + 2 * p + 1 : base + 2 * p + 2])
        )
    return jnp.concatenate(parts, axis=1)


def half_silu(h):
    return h + h * jnp.tanh(h)


def ssm_kernel(
    buf, cw, cb, rate, skip, y, raw, rawbc, cum_s, row_s, end_s, tot_s, x_s, c_s, b_s, carry_s
):
    tm = lax.axis_index("tm")
    col0 = pl.multiple_of(tm * WIDE, WIDE)

    raw_steps = buf[:, 2 * GROUP :, :GROUP].astype(jnp.float32).reshape(BLOCKS * 8, GROUP)
    z = jnp.exp(-jnp.abs(raw_steps))
    u = 1.0 + z
    log1p = jnp.where(u == 1.0, z, jnp.log(u) * (z / jnp.where(u == 1.0, 1.0, u - 1.0)))
    dt = jnp.maximum(raw_steps, 0.0) + log1p
    sub = lax.broadcasted_iota(jnp.int32, (BLOCKS * 8, GROUP), 0) % 8
    rates = jnp.zeros((BLOCKS * 8, GROUP), jnp.float32)
    for k in range(8):
        rates = jnp.where(sub == k, rate[k // OWN, tm * OWN + k % OWN], rates)
    decay = dt * rates * (-LOG2E)
    ri = lax.broadcasted_iota(jnp.int32, (GROUP, GROUP), 0)
    ci = lax.broadcasted_iota(jnp.int32, (GROUP, GROUP), 1)
    prefix = jnp.dot(decay, (ri <= ci).astype(jnp.float32), precision=lax.Precision.HIGHEST)
    suffix = jnp.dot(decay, (ri >= ci).astype(jnp.float32), precision=lax.Precision.HIGHEST)
    is_fwd = sub < OWN
    cum = jnp.where(is_fwd, prefix, suffix)
    total = jnp.where(is_fwd[:, :1], prefix[:, GROUP - 1 :], suffix[:, :1])
    row = cum - jnp.log(dt) * LOG2E
    row_s[...] = row
    tot_s[...] = jnp.broadcast_to(jnp.exp2(total), (BLOCKS * 8, GROUP))
    cum_s[...] = cum.T
    end_s[...] = jnp.exp2(total - row).T

    for ref in (raw, rawbc):
        ref[0:8] = jnp.zeros((8, WIDE), jnp.float32)
        ref[8 + BLOCKS * GROUP :] = jnp.zeros((8, WIDE), jnp.float32)

    def widen(i, _):
        at = pl.ds(pl.multiple_of(8 + i * GROUP, 8), GROUP)
        raw[at] = buf[i, :GROUP].astype(jnp.float32)
        rawbc[at] = buf[i, GROUP : 2 * GROUP].astype(jnp.float32)
        return 0

    lax.fori_loop(0, BLOCKS, widen, 0)

    weights = [[cw[d, pl.ds(k, 1), pl.ds(col0, WIDE)] * 0.5 for k in range(4)] for d in range(2)]
    bias = [cb[pl.ds(d, 1), pl.ds(col0, WIDE)] * 0.5 for d in range(2)]
    weights_bc = [[cw[d, pl.ds(k, 1), INNER:] * 0.5 for k in range(4)] for d in range(2)]
    bias_bc = [cb[pl.ds(d, 1), INNER:] * 0.5 for d in range(2)]
    low = lax.broadcasted_iota(jnp.int32, (GROUP, 128), 1) < STATE

    def shifted(window, s):
        if s == 0:
            return window[8 : 8 + GROUP]
        return pltpu.roll(window, GROUP + 16 - (8 + s), 0)[:GROUP]

    def conv(window, d, taps, offset):
        sign = 1 if d == 0 else -1
        acc = offset + taps[3] * shifted(window, 0)
        for k in range(3):
            acc = acc + taps[k] * shifted(window, sign * (k - 3))
        return half_silu(acc)

    def convolve(i, _):
        at = pl.ds(pl.multiple_of(i * GROUP, GROUP), GROUP + 16)
        window, window_bc = raw[at], rawbc[at]
        for d in range(2):
            x_s[d, i] = conv(window, d, weights[d], bias[d]).astype(jnp.bfloat16)
            bc = conv(window_bc[:, d * 128 : (d + 1) * 128], d, weights_bc[d], bias_bc[d])
            bc = bc.astype(jnp.bfloat16).astype(jnp.float32)
            c_s[d, i] = jnp.where(low, pltpu.roll(bc, STATE, 1), bc).astype(jnp.bfloat16)
            b_s[d, i] = jnp.where(low, bc, 0.0).astype(jnp.bfloat16)
        return 0

    lax.fori_loop(0, BLOCKS, convolve, 0)

    def scan(i, carries):
        new = []
        for d in range(2):
            at = i if d == 0 else BLOCKS - 1 - i
            carry = carries[d]
            high = carry.astype(jnp.bfloat16)
            carry_s[d, at, :STATE] = high
            carry_s[d, at, STATE:] = (carry - high.astype(jnp.float32)).astype(jnp.bfloat16)
            ends = pltpu.roll(end_s[...], (GROUP - 8 * at) % GROUP, 1)
            scaled = (x_s[d, at].astype(jnp.float32) * spread(ends, d * OWN)).astype(jnp.bfloat16)
            state = lax.dot_general(
                b_s[d, at], scaled, (((0,), (0,)), ((), ())), preferred_element_type=jnp.float32
            )[:STATE]
            rows = tot_s[pl.ds(pl.multiple_of(8 * at, 8), 8)]
            new.append(spread_row(rows, d * OWN) * carry + state)
        return tuple(new)

    zero = jnp.zeros((STATE, WIDE), jnp.float32)
    lax.fori_loop(0, BLOCKS, scan, (zero, zero))

    lane = lax.broadcasted_iota(jnp.int32, (1, WIDE), 1) // HEADDIM
    skips = []
    for d in range(2):
        value = jnp.zeros((1, WIDE), jnp.float32)
        for h in range(OWN):
            value = jnp.where(lane == h, skip[d, tm * OWN + h], value)
        skips.append(value)

    def outputs(i, _):
        cums = pltpu.roll(cum_s[...], (GROUP - 8 * i) % GROUP, 1)
        rows = row_s[pl.ds(pl.multiple_of(8 * i, 8), 8)]
        decays = jnp.exp2(cums)
        x = [x_s[d, i] for d in range(2)]
        wide = jnp.zeros((GROUP, WIDE), jnp.float32)
        scores = []
        for d in range(2):
            score = lax.dot_general(
                c_s[d, i], b_s[d, i], (((1,), (1,)), ((), ())), preferred_element_type=jnp.float32
            )
            scores.append(jnp.where((ri >= ci) if d == 0 else (ri <= ci), score, 0.0))
            carried = jnp.dot(c_s[d, i], carry_s[d, i], preferred_element_type=jnp.float32)
            wide = wide + carried * spread(decays, d * OWN) + skips[d] * x[d].astype(jnp.float32)
        for p in range(OWN // 2):
            left, right = [], []
            for q in range(2):
                for d in range(2):
                    k = d * OWN + 2 * p + q
                    grow = jnp.exp2(jnp.minimum(cums[:, k : k + 1] - rows[k : k + 1], 64.0))
                    left.append((grow * scores[d]).astype(jnp.bfloat16))
                    pair = x[d][:, p * 128 : (p + 1) * 128]
                    keep = low if q == 0 else jnp.logical_not(low)
                    right.append(jnp.where(keep, pair, jnp.zeros_like(pair)))
            local = jnp.dot(
                jnp.concatenate(left, axis=1),
                jnp.concatenate(right, axis=0),
                preferred_element_type=jnp.float32,
            )
            y[i, :, p * 128 : (p + 1) * 128] = local + wide[:, p * 128 : (p + 1) * 128]
        return 0

    lax.fori_loop(0, BLOCKS, outputs, 0)


def gate_kernel(y, gate, gated, sums):
    def one(i, _):
        g = y[i] * half_silu(gate[i].astype(jnp.float32) * 0.5)
        gated[i] = g
        total = lax.dot_general(
            jnp.ones((8, WIDE), jnp.float32),
            g * g,
            (((1,), (1,)), ((), ())),
            precision=lax.Precision.HIGHEST,
            preferred_element_type=jnp.float32,
        )
        sums[:, pl.ds(i, 1), :] = jnp.broadcast_to(total[:1][None], (BLOCKS, 1, GROUP))
        return 0

    lax.fori_loop(0, BLOCKS, one, 0)


def norm_kernel(gated, sums, gain, out, inv_s):
    gains = gain[0:1, pl.ds(pl.multiple_of(lax.axis_index("tm") * WIDE, WIDE), WIDE)]
    total = sums[0]
    for k in range(1, BLOCKS):
        total = total + sums[k]
    inv = lax.rsqrt(total * (1.0 / INNER) + EPSILON)
    inv_s[...] = jnp.concatenate(
        [inv, jnp.zeros((GROUP - BLOCKS, GROUP), jnp.float32)], axis=0
    ).T

    def one(i, _):
        scale = pltpu.roll(inv_s[...], (GROUP - i) % GROUP, 1)[:, :1]
        out[i] = (gated[i] * scale * gains).astype(jnp.bfloat16)
        return 0

    lax.fori_loop(0, BLOCKS, one, 0)


def swap(array, axis):
    return lax.all_to_all(array, axis, split_axis=0, concat_axis=0, tiled=True)


def shards(
    signal,
    gate_input,
    bc_forward,
    bc_backward,
    step_raw,
    decay_rate,
    conv_weight,
    conv_bias,
    skip_gain,
    norm_gain,
):
    f32, bf16 = jnp.float32, jnp.bfloat16
    packed = pl.pallas_call(
        pack_kernel,
        out_shape=jax.ShapeDtypeStruct((BLOCKS, ROWS, WIDE), bf16),
        in_specs=[VMEM] * 4,
        out_specs=VMEM,
        name="pack",
        cost_estimate=pl.CostEstimate(flops=0, bytes_accessed=4 << 20, transcendentals=0),
    )(signal, bc_forward, bc_backward, step_raw)
    got = swap(packed, "tm")
    gates = gate_input[0].reshape(GROUP, BLOCKS, WIDE).transpose(1, 0, 2)
    gates = swap(gates, "tm")
    y = pl.pallas_call(
        ssm_kernel,
        out_shape=jax.ShapeDtypeStruct((BLOCKS, GROUP, WIDE), f32),
        in_specs=[VMEM, VMEM, VMEM, SMEM, SMEM],
        out_specs=VMEM,
        scratch_shapes=[
            pltpu.VMEM((BLOCKS * GROUP + 16, WIDE), f32),
            pltpu.VMEM((BLOCKS * GROUP + 16, WIDE), f32),
            pltpu.VMEM((GROUP, BLOCKS * 8), f32),
            pltpu.VMEM((BLOCKS * 8, GROUP), f32),
            pltpu.VMEM((GROUP, BLOCKS * 8), f32),
            pltpu.VMEM((BLOCKS * 8, GROUP), f32),
            pltpu.VMEM((2, BLOCKS, GROUP, WIDE), bf16),
            pltpu.VMEM((2, BLOCKS, GROUP, 128), bf16),
            pltpu.VMEM((2, BLOCKS, GROUP, 128), bf16),
            pltpu.VMEM((2, BLOCKS, 2 * STATE, WIDE), bf16),
        ],
        name="ssm",
        cost_estimate=pl.CostEstimate(
            flops=20_000_000_000, bytes_accessed=8 << 20, transcendentals=4_000_000
        ),
    )(got, conv_weight, conv_bias, decay_rate, skip_gain)
    gated, sums = pl.pallas_call(
        gate_kernel,
        out_shape=(
            jax.ShapeDtypeStruct((BLOCKS, GROUP, WIDE), f32),
            jax.ShapeDtypeStruct((BLOCKS, BLOCKS, GROUP), f32),
        ),
        in_specs=[VMEM] * 2,
        out_specs=(VMEM, VMEM),
        name="gate",
    )(y, gates)
    sums = swap(sums, "tm")
    normed = pl.pallas_call(
        norm_kernel,
        out_shape=jax.ShapeDtypeStruct((BLOCKS, GROUP, WIDE), bf16),
        in_specs=[VMEM] * 3,
        out_specs=VMEM,
        scratch_shapes=[pltpu.VMEM((GROUP, GROUP), f32)],
        name="norm",
    )(gated, sums, norm_gain[None])
    return swap(normed, "batch")


def solution(mesh):
    in_specs = (
        P("batch", "tm", None),
        P("batch", "tm", None),
        P("batch", "tm", None),
        P("batch", "tm", None),
        P("batch", "tm", None),
        P(),
        P(),
        P(),
        P(),
        P(),
    )
    out_specs = P(None, "batch", "tm")
    return jax.shard_map(shards, mesh=mesh, in_specs=in_specs, out_specs=out_specs, check_vma=False)
```

time: 474 us -> 136 us (0.29)
  waiting for transfers between devices: 191 us -> 23.9 us
  other arithmetic: 97.9 us -> 0 us
  local copies, waits for them, and re-layouts: 54.4 us -> 4.87 us
  Pallas kernels: 0 us -> 41.4 us
  blocking collectives: 92.6 us -> 52.4 us
  between operations: 14 us -> 0.02 us
  matrix products: 12.7 us -> 0 us
  starting transfers between devices: 6.51 us -> 12.6 us
    all_gather x2 -> x0, waiting for transfers between devices: 190 us -> none  [the longest x1 134 us: entering(): pieces = jax.tree.map(lambda part: lax.all_gather(part, axis), value)]
    pallas_call x0 -> x4, Pallas kernels: none -> 41.4 us  [the longest x1 26.6 us: shards(): pl.pallas_call(ssm_kernel, out_shape=jax.ShapeDtypeStruct((BLOCKS, GROUP,...]
    all_gather x2 -> x0, blocking collectives: 33.2 us -> none  [the longest x1 16.9 us: carried_in(): lax.all_gather(a.astype(kind), axis)]
    unnamed x3 -> x0, other arithmetic: 33 us -> none
    select_n x15 -> x0, other arithmetic: 31.2 us -> none  [lap(): jnp.where(position < mine, new, old)]
    all_to_all x0 -> x2, waiting for transfers between devices: none -> 23.9 us  [swap(): return lax.all_to_all(array, axis, split_axis=0, concat_axis=0, tiled=True)]
    add x11 -> x0, other arithmetic: 19.2 us -> none  [combine(): earlier[1] * later[0][:, None, None] + later[1]]
    rev x4 -> x0, local copies, waits for them, and re-layouts: 14 us -> none  [the longest x1 12.6 us: shards(): backward_out = block_outputs(bwd_parts, bwd_in[1], skip_gain[1])[::-1]]
  transfers between devices with their start and end apart: 4 -> 2, of which waited for: 2 -> 1; matrix products, arithmetic and copies ran while one was open for 13% -> 2% of each run, Pallas kernels for 0% -> 20%
where the time goes in v1:
time: 136 us; the launch traced here: 135 us
  blocking collectives  52.4 us (39%)
  Pallas kernels  41.4 us (30%)
  waiting for transfers between devices  23.9 us (18%)
  starting transfers between devices  12.6 us (9%)
  local copies, waits for them, and re-layouts  4.87 us (4%)
    all_to_all x2, blocking collectives, swap(): return lax.all_to_all(array, axis, split_axis=0, concat_axis=0, tiled=True)  52.4 us
    pallas_call x1, Pallas kernels, shards(): pl.pallas_call(ssm_kernel, out_shape=jax.ShapeDtypeStruct((BLOCKS, GROUP,...  26.6 us
    all_to_all x2, waiting for transfers between devices, swap(): return lax.all_to_all(array, axis, split_axis=0, concat_axis=0, tiled=True)  23.9 us
    all_to_all x2, starting transfers between devices, swap(): return lax.all_to_all(array, axis, split_axis=0, concat_axis=0, tiled=True)  12.6 us
    pallas_call x1, Pallas kernels, shards(): pl.pallas_call(gate_kernel, out_shape=(jax.ShapeDtypeStruct((BLOCKS, GROU...  6.8 us
    pallas_call x1, Pallas kernels, shards(): pl.pallas_call(norm_kernel, out_shape=jax.ShapeDtypeStruct((BLOCKS, GROUP...  5.33 us
    unnamed x6, local copies, waits for them, and re-layouts  3.56 us
    pallas_call x1, Pallas kernels, shards(): pl.pallas_call(pack_kernel, out_shape=jax.ShapeDtypeStruct((BLOCKS, ROWS,...  2.75 us
  transfers between devices with their start and end apart: 2, of which 1 were waited for; matrix products, arithmetic and copies ran while one was open for 2% of the time, Pallas kernels for 20%

profile of v1, /device:TPU:2, one launch (start us, length us, event | category | flops | bytes accessed | tf_op | source)
XLA Modules:
  0.0 135.2 jit_solution(11923314481737886195)
XLA Ops:
  0.0 2.8 %pack.1 = bf16[16,264,256]{2,1,0:T(8,128)(2,1)} custom-call(bf16[1,128,4096]{2,1,0:T(8,128)(2,1)} %signal.1, bf16[1,128,128]{2,1,0:T(8,128)(2,1)} %bcf.1, bf16[1,128,128]{2,1,0:T(8,128)(2,1)} %bcb.1, bf16[1,128,128]{2,1,0:T(8,128)(2,1)} %step.1), custom_call_target="tpu_custom_call" | custom-call | bytes 4194304 | tf_op jit(solution)/shard_map/pack/pallas_call | solution.py:250
  2.8 5.9 %all-to-all-start = ((bf16[16,264,256]{2,1,0:T(8,128)(2,1)}), bf16[16,264,256]{2,1,0:T(8,128)(2,1)S(1)}, u32[]{:S(2)}, u32[]{:S(2)}) async-start(bf16[16,264,256]{2,1,0:T(8,128)(2,1)} %pack.1), calls=%async_computation | async-start | bytes 4325376 | tf_op jit(solution)/shard_map/all_to_all | solution.py:234
  8.6 1.6 %copy.11 = bf16[1,128,4096]{1,2,0:T(8,128)(2,1)S(1)} copy(bf16[1,128,4096]{2,1,0:T(8,128)(2,1)} %param.11) | data formatting | bytes 2097152 | tf_op args[1]
  10.2 1.3 copy.12
  11.5 23.9 %all-to-all-done.buf = bf16[16,264,256]{2,1,0:T(8,128)(2,1)S(1)} async-done(((bf16[16,264,256]{2,1,0:T(8,128)(2,1)}), bf16[16,264,256]{2,1,0:T(8,128)(2,1)S(1)}, u32[]{:S(2)}, u32[]{:S(2)}) %all-to-all-start) | async-done | bytes 2162720 | tf_op jit(solution)/shard_map/all_to_all | solution.py:234
  35.4 0.0 copy-start.1
  35.4 6.7 %all-to-all-start.1 = ((bf16[16,128,256]{2,1,0:T(8,128)(2,1)}), bf16[16,128,256]{2,1,0:T(8,128)(2,1)S(1)}, u32[]{:S(2)}, u32[]{:S(2)}) async-start(bf16[16,128,256]{2,1,0:T(8,128)(2,1)} %bitcast.1), calls=%async_computation.1 | async-start | bytes 2097152 | tf_op jit(solution)/shard_map/all_to_all | solution.py:234
  42.1 0.0 copy-done.1
  42.2 26.6 %ssm.1.y = f32[16,128,256]{2,1,0:T(8,128)} custom-call(bf16[16,264,256]{2,1,0:T(8,128)(2,1)} %copy-done.1, f32[2,4,4224]{2,1,0:T(4,128)} %cw.1, f32[2,4224]{1,0:T(2,128)} %cb.1, f32[2,64]{1,0:T(2,128)} %rate.1, f32[2,64]{1,0:T(2,128)} %skip.1), custom_call_target="tpu_custom_call" | custom-call | flops 20000000000 | bytes 8388608 | tf_op jit(solution)/shard_map/ssm/pallas_call | solution.py:261
  68.7 0.0 all-to-all-done.1.gate
  68.7 0.0 copy-start
  68.7 1.0 copy-done
  69.7 6.8 %gate.1 = (f32[16,128,256]{2,1,0:T(8,128)}, f32[16,16,128]{2,1,0:T(8,128)}) custom-call(f32[16,128,256]{2,1,0:T(8,128)} %ssm.1.y, bf16[16,128,256]{2,1,0:T(8,128)(2,1)} %copy-done), custom_call_target="tpu_custom_call" | custom-call | tf_op jit(solution)/shard_map/gate/pallas_call | solution.py:283
  76.5 10.7 %all_to_all.20.sums = f32[16,16,128]{2,1,0:T(8,128)} all-to-all(f32[16,16,128]{2,1,0:T(8,128)} %get-tuple-element.8), channel_id=1, replica_groups=mesh['tm'=16,'batch'=16] {'tm'}, dimensions={0} | all-to-all | bytes 262144 | tf_op jit(solution)/shard_map/all_to_all | solution.py:234
  87.2 5.3 %norm.1 = bf16[16,128,256]{2,1,0:T(8,128)(2,1)} custom-call(f32[16,128,256]{2,1,0:T(8,128)} %get-tuple-element.7.gated, f32[16,16,128]{2,1,0:T(8,128)} %all_to_all.20.sums, f32[1,4096]{1,0:T(1,128)} %bitcast.4), custom_call_target="tpu_custom_call" | custom-call | tf_op jit(solution)/shard_map/norm/pallas_call | solution.py:294
  92.5 41.7 %all_to_all.21 = bf16[16,128,256]{2,1,0:T(8,128)(2,1)S(1)} all-to-all(bf16[16,128,256]{2,1,0:T(8,128)(2,1)} %norm.1), channel_id=1, replica_groups=mesh['tm'=16,'batch'=16] {'batch'}, dimensions={0} | all-to-all | bytes 2097152 | tf_op jit(solution)/shard_map/all_to_all | solution.py:234
  134.2 1.0 copy.14
Async XLA Ops:
  2.8 32.7 %all-to-all-start = ((bf16[16,264,256]{2,1,0:T(8,128)(2,1)}), bf16[16,264,256]{2,1,0:T(8,128)(2,1)S(1)}, u32[]{:S(2)}, u32[]{:S(2)}) async-start(bf16[16,264,256]{2,1,0:T(8,128)(2,1)} %pack.1), calls=%async_computation | async-start | bytes 4325376 | tf_op jit(solution)/shard_map/all_to_all | solution.py:234
  35.4 6.7 %copy-start.1 = (bf16[16,264,256]{2,1,0:T(8,128)(2,1)}, bf16[16,264,256]{2,1,0:T(8,128)(2,1)S(1)}, u32[]{:S(2)}) copy-start(bf16[16,264,256]{2,1,0:T(8,128)(2,1)S(1)} %all-to-all-done.buf) | copy-start | bytes 6488068
  35.4 33.3 %all-to-all-start.1 = ((bf16[16,128,256]{2,1,0:T(8,128)(2,1)}), bf16[16,128,256]{2,1,0:T(8,128)(2,1)S(1)}, u32[]{:S(2)}, u32[]{:S(2)}) async-start(bf16[16,128,256]{2,1,0:T(8,128)(2,1)} %bitcast.1), calls=%async_computation.1 | async-start | bytes 2097152 | tf_op jit(solution)/shard_map/all_to_all | solution.py:234
  68.7 1.0 copy-start

commit v2 on v1

v2 whole, which is shorter than its diff:
```python
import functools

import jax
import jax.numpy as jnp
from jax import lax
from jax.experimental import pallas as pl
from jax.experimental.pallas import tpu as pltpu
from jax.sharding import PartitionSpec as P

INNER = 4096
HEADDIM = 64
STATE = 64
GROUP = 128
HEADS = 64
BLOCKS = 16
OWN = 4
WIDE = OWN * HEADDIM
ROWS = 2 * GROUP + 8
EPSILON = 1e-05
UNROLL_BC, UNROLL_X, UNROLL_Y = 2, 2, 2
LOG2E = 1.4426950408889634
VMEM = pl.BlockSpec(memory_space=pltpu.VMEM)
SMEM = pl.BlockSpec(memory_space=pltpu.SMEM)


def pack_kernel(signal, bcf, bcb, step, out):
    both = jnp.concatenate([bcf[0], bcb[0]], axis=1)
    steps = step[0].astype(jnp.float32).T
    for c in range(BLOCKS):
        out[c, :GROUP] = signal[0, :, c * WIDE : (c + 1) * WIDE]
        out[c, GROUP : 2 * GROUP] = both
        mine = jnp.concatenate(
            [steps[c * OWN : (c + 1) * OWN], steps[HEADS + c * OWN : HEADS + (c + 1) * OWN]], axis=0
        )
        out[c, 2 * GROUP :] = jnp.concatenate([mine, jnp.zeros_like(mine)], axis=1).astype(
            jnp.bfloat16
        )


def half_silu(h):
    return h + h * jnp.tanh(h)


def pieces(value):
    parts = []
    for _ in range(3):
        part = value.astype(jnp.bfloat16).astype(jnp.float32)
        parts.append(part)
        value = value - part
    return parts


def ssm_kernel(
    buf, cw, cb, rate, skip, y, raw, row_s, cum_s, dec_s, end_s, tot_s, fixed_s, x_s, c_s, bt_s, btb_s, st_s, carry_s
):
    f32, bf16 = jnp.float32, jnp.bfloat16
    tm = lax.axis_index("tm")
    n8 = BLOCKS * 8

    raw_steps = buf[:, 2 * GROUP :, :GROUP].astype(f32).reshape(n8, GROUP)
    z = jnp.exp(-jnp.abs(raw_steps))
    u = 1.0 + z
    log1p = jnp.where(u == 1.0, z, jnp.log(u) * (z / jnp.where(u == 1.0, 1.0, u - 1.0)))
    dt = jnp.maximum(raw_steps, 0.0) + log1p
    sub = lax.broadcasted_iota(jnp.int32, (8, GROUP), 0)
    rates = jnp.zeros((8, GROUP), f32)
    for k in range(8):
        rates = jnp.where(sub == k, rate[k // OWN, tm * OWN + k % OWN], rates)
    decay = (dt.reshape(BLOCKS, 8, GROUP) * (rates * (-LOG2E))[None]).reshape(n8, GROUP)
    ri = lax.broadcasted_iota(jnp.int32, (GROUP, GROUP), 0)
    ci = lax.broadcasted_iota(jnp.int32, (GROUP, GROUP), 1)
    sums = jnp.concatenate([(ri <= ci).astype(f32), (ri >= ci).astype(f32)], axis=1).astype(bf16)
    both = jnp.dot(
        jnp.concatenate(pieces(decay), axis=1).astype(bf16),
        jnp.concatenate([sums] * 3, axis=0),
        preferred_element_type=f32,
    )
    prefix, suffix = both[:, :GROUP], both[:, GROUP:]
    is_fwd = lax.broadcasted_iota(jnp.int32, (n8, GROUP), 0) % 8 < OWN
    cum = jnp.where(is_fwd, prefix, suffix)
    total = jnp.where(is_fwd[:, :1], prefix[:, GROUP - 1 :], suffix[:, :1])
    row = cum - jnp.log(dt) * LOG2E
    row_s[...] = -row
    cum_s[...] = cum
    dec_s[...] = jnp.exp2(cum)
    end_s[...] = jnp.exp2(total - row)
    tot_s[...] = jnp.broadcast_to(jnp.exp2(total), (n8, GROUP))

    low = lax.broadcasted_iota(jnp.int32, (GROUP, 128), 1) < HEADDIM
    sub128 = lax.broadcasted_iota(jnp.int32, (96, 128), 0)
    for k in range(12):
        if k < 8:
            chosen = (sub128 < 24) & (sub128 % 8 == k)
        else:
            d, p = divmod(k - 8, 2)
            head = d * OWN + 2 * p + jnp.where(low[:96], 0, 1)
            chosen = (sub128 >= 32) & (sub128 < 56) & (sub128 % 8 == head)
        fixed_s[k] = jnp.where(chosen, 1.0, 0.0).astype(bf16)

    for t in range(4):
        raw[t, 0:8] = jnp.zeros((8, 128), f32)
        raw[t, 8 + BLOCKS * GROUP :] = jnp.zeros((8, 128), f32)

    def widen(i, _):
        at = pl.ds(pl.multiple_of(8 + i * GROUP, 8), GROUP)
        for t in range(4):
            top = (t // 2) * GROUP
            raw[t, at] = buf[i, top : top + GROUP, (t % 2) * 128 : (t % 2 + 1) * 128].astype(f32)
        return 0

    lax.fori_loop(0, BLOCKS, widen, 0)

    def conv(t, i, d, taps, offset):
        sign = 1 if d == 0 else -1
        acc = offset
        for k in range(4):
            acc = acc + taps[k] * raw[t, pl.ds(i * GROUP + (8 + sign * (k - 3)), GROUP)]
        return half_silu(acc)

    def taps_of(d, lanes):
        return [cw[d, pl.ds(k, 1), lanes] * 0.5 for k in range(4)], cb[pl.ds(d, 1), lanes] * 0.5

    for d in range(2):
        taps, offset = taps_of(d, slice(INNER, INNER + 128))

        def convolve_bc(j, _):
            for e in range(UNROLL_BC):
                i = j * UNROLL_BC + e
                bc = conv(2 + d, i, d, taps, offset).astype(bf16).astype(f32)
                c_s[d, i] = jnp.where(low, pltpu.roll(bc, STATE, 1), bc).astype(bf16)
                turned = bc.T[:STATE]
                bt_s[d, i] = turned
                btb_s[d, i] = turned.astype(bf16)
            return 0

        lax.fori_loop(0, BLOCKS // UNROLL_BC, convolve_bc, 0)

    for p in range(OWN // 2):
        lanes = pl.ds(pl.multiple_of(tm * WIDE + p * 128, 128), 128)
        filters = [taps_of(d, lanes) for d in range(2)]

        def convolve(j, _):
            for e in range(UNROLL_X):
                i = j * UNROLL_X + e
                ends = end_s[pl.ds(pl.multiple_of(8 * i, 8), 8)]
                for d in range(2):
                    x = conv(p, i, d, *filters[d]).astype(bf16)
                    x_s[d, p, i] = x
                    k = d * OWN + 2 * p
                    turned = bt_s[d, i]
                    scaled = jnp.concatenate(
                        [turned * ends[k : k + 1], turned * ends[k + 1 : k + 2]], axis=0
                    ).astype(bf16)
                    state = jnp.dot(scaled, x, preferred_element_type=f32)
                    st_s[d, p, i] = jnp.where(low[:STATE], state[:STATE], state[STATE:])
            return 0

        lax.fori_loop(0, BLOCKS // UNROLL_X, convolve, 0)

    def scan(i, carries):
        new = []
        for d in range(2):
            at = i if d == 0 else BLOCKS - 1 - i
            rows = tot_s[pl.ds(pl.multiple_of(8 * at, 8), 8)]
            for p in range(OWN // 2):
                carry = carries[2 * d + p]
                high = carry.astype(bf16)
                lanes = slice(p * 128, (p + 1) * 128)
                carry_s[d, at, :STATE, lanes] = high
                carry_s[d, at, STATE:, lanes] = (carry - high.astype(f32)).astype(bf16)
                k = d * OWN + 2 * p
                keep = jnp.where(low[:1], rows[k : k + 1], rows[k + 1 : k + 2])
                new.append(keep * carry + st_s[d, p, at])
        return tuple(new)

    lax.fori_loop(0, BLOCKS, scan, tuple(jnp.zeros((STATE, 128), f32) for _ in range(4)))

    skips = []
    for d in range(2):
        for p in range(OWN // 2):
            at = tm * OWN + 2 * p
            skips.append(jnp.where(low[:1], skip[d, at], skip[d, at + 1]))
    sub32 = lax.broadcasted_iota(jnp.int32, (32, GROUP), 0)
    ones = jnp.where(sub32 < 24, 1.0, 0.0)
    blank = jnp.zeros((8, GROUP), f32)

    def one_block(i):
        at = pl.ds(pl.multiple_of(8 * i, 8), 8)
        left = jnp.concatenate(
            [ones, *pieces(cum_s[at]), blank, *pieces(dec_s[at]), blank, jnp.zeros((32, GROUP), f32)],
            axis=0,
        ).T.astype(bf16)
        rows = jnp.concatenate([*pieces(row_s[at]), blank], axis=0)
        right = []
        for k in range(12):
            part = jnp.where(sub32 % 8 == k, rows, 0.0) if k < 8 else jnp.zeros((32, GROUP), f32)
            right.append(jnp.concatenate([part.astype(bf16), fixed_s[k]], axis=0))
        grid = jnp.dot(left, jnp.concatenate(right, axis=1), preferred_element_type=f32)
        scores, wide = [], [0.0, 0.0]
        for d in range(2):
            c = c_s[d, i]
            score = jnp.dot(c[:, :STATE], btb_s[d, i], preferred_element_type=f32)
            scores.append(jnp.where((ri >= ci) if d == 0 else (ri <= ci), score, 0.0))
            carried = jnp.dot(c, carry_s[d, i], preferred_element_type=f32)
            for p in range(OWN // 2):
                lanes = slice(p * 128, (p + 1) * 128)
                decays = grid[:, (8 + 2 * d + p) * 128 : (9 + 2 * d + p) * 128]
                wide[p] = (
                    wide[p] + carried[:, lanes] * decays + skips[2 * d + p] * x_s[d, p, i].astype(f32)
                )
        for p in range(OWN // 2):
            heads = []
            for q in range(2):
                parts = []
                for d in range(2):
                    k = d * OWN + 2 * p + q
                    grow = jnp.exp2(jnp.minimum(grid[:, k * 128 : (k + 1) * 128], 64.0))
                    parts.append((grow * scores[d]).astype(bf16))
                heads.append(jnp.concatenate(parts, axis=1))
            local = jnp.dot(
                jnp.concatenate(heads, axis=0),
                jnp.concatenate([x_s[0, p, i], x_s[1, p, i]], axis=0),
                preferred_element_type=f32,
            )
            local = jnp.where(low, local[:GROUP], local[GROUP:])
            y[i, :, p * 128 : (p + 1) * 128] = local + wide[p]

    def outputs(j, _):
        for e in range(UNROLL_Y):
            one_block(j * UNROLL_Y + e)
        return 0

    lax.fori_loop(0, BLOCKS // UNROLL_Y, outputs, 0)


def gate_kernel(y, gate, gated, sums):
    def one(i, _):
        g = y[i] * half_silu(gate[i].astype(jnp.float32) * 0.5)
        gated[i] = g
        total = lax.dot_general(
            jnp.ones((8, WIDE), jnp.float32),
            g * g,
            (((1,), (1,)), ((), ())),
            precision=lax.Precision.HIGHEST,
            preferred_element_type=jnp.float32,
        )
        sums[:, pl.ds(i, 1), :] = jnp.broadcast_to(total[:1][None], (BLOCKS, 1, GROUP))
        return 0

    lax.fori_loop(0, BLOCKS, one, 0)


def norm_kernel(gated, sums, gain, out, inv_s):
    gains = gain[0:1, pl.ds(pl.multiple_of(lax.axis_index("tm") * WIDE, WIDE), WIDE)]
    total = sums[0]
    for k in range(1, BLOCKS):
        total = total + sums[k]
    inv = lax.rsqrt(total * (1.0 / INNER) + EPSILON)
    inv_s[...] = jnp.concatenate(
        [inv, jnp.zeros((GROUP - BLOCKS, GROUP), jnp.float32)], axis=0
    ).T

    def one(i, _):
        scale = pltpu.roll(inv_s[...], (GROUP - i) % GROUP, 1)[:, :1]
        out[i] = (gated[i] * scale * gains).astype(jnp.bfloat16)
        return 0

    lax.fori_loop(0, BLOCKS, one, 0)


def swap(array, axis):
    return lax.all_to_all(array, axis, split_axis=0, concat_axis=0, tiled=True)


def shards(
    signal,
    gate_input,
    bc_forward,
    bc_backward,
    step_raw,
    decay_rate,
    conv_weight,
    conv_bias,
    skip_gain,
    norm_gain,
):
    f32, bf16 = jnp.float32, jnp.bfloat16
    packed = pl.pallas_call(
        pack_kernel,
        out_shape=jax.ShapeDtypeStruct((BLOCKS, ROWS, WIDE), bf16),
        in_specs=[VMEM] * 4,
        out_specs=VMEM,
        name="pack",
        cost_estimate=pl.CostEstimate(flops=0, bytes_accessed=4 << 20, transcendentals=0),
    )(signal, bc_forward, bc_backward, step_raw)
    got = swap(packed, "tm")
    gates = gate_input[0].reshape(GROUP, BLOCKS, WIDE).transpose(1, 0, 2)
    gates = swap(gates, "tm")
    y = pl.pallas_call(
        ssm_kernel,
        out_shape=jax.ShapeDtypeStruct((BLOCKS, GROUP, WIDE), f32),
        in_specs=[VMEM, VMEM, VMEM, SMEM, SMEM],
        out_specs=VMEM,
        scratch_shapes=[
            pltpu.VMEM((4, BLOCKS * GROUP + 16, 128), f32),
            *[pltpu.VMEM((BLOCKS * 8, GROUP), f32)] * 5,
            pltpu.VMEM((12, 96, 128), bf16),
            pltpu.VMEM((2, 2, BLOCKS, GROUP, 128), bf16),
            pltpu.VMEM((2, BLOCKS, GROUP, 128), bf16),
            pltpu.VMEM((2, BLOCKS, STATE, 128), f32),
            pltpu.VMEM((2, BLOCKS, STATE, 128), bf16),
            pltpu.VMEM((2, 2, BLOCKS, STATE, 128), f32),
            pltpu.VMEM((2, BLOCKS, 2 * STATE, WIDE), bf16),
        ],
        name="ssm",
        cost_estimate=pl.CostEstimate(
            flops=20_000_000_000, bytes_accessed=8 << 20, transcendentals=4_000_000
        ),
    )(got, conv_weight, conv_bias, decay_rate, skip_gain)
    gated, sums = pl.pallas_call(
        gate_kernel,
        out_shape=(
            jax.ShapeDtypeStruct((BLOCKS, GROUP, WIDE), f32),
            jax.ShapeDtypeStruct((BLOCKS, BLOCKS, GROUP), f32),
        ),
        in_specs=[VMEM] * 2,
        out_specs=(VMEM, VMEM),
        name="gate",
    )(y, gates)
    sums = swap(sums, "tm")
    normed = pl.pallas_call(
        norm_kernel,
        out_shape=jax.ShapeDtypeStruct((BLOCKS, GROUP, WIDE), bf16),
        in_specs=[VMEM] * 3,
        out_specs=VMEM,
        scratch_shapes=[pltpu.VMEM((GROUP, GROUP), f32)],
        name="norm",
    )(gated, sums, norm_gain[None])
    return swap(normed, "batch")


def solution(mesh):
    in_specs = (
        P("batch", "tm", None),
        P("batch", "tm", None),
        P("batch", "tm", None),
        P("batch", "tm", None),
        P("batch", "tm", None),
        P(),
        P(),
        P(),
        P(),
        P(),
    )
    out_specs = P(None, "batch", "tm")
    return jax.shard_map(shards, mesh=mesh, in_specs=in_specs, out_specs=out_specs, check_vma=False)
```

time: 136 us -> 127 us (0.934)
  Pallas kernels: 41.4 us -> 32.3 us
    pallas_call x1, Pallas kernels: 26.6 us -> 17.4 us  [shards(): pl.pallas_call(ssm_kernel, out_shape=jax.ShapeDtypeStruct((BLOCKS, GROUP,...]
  transfers between devices with their start and end apart: 2 -> 2, of which waited for: 1 -> 1; matrix products, arithmetic and copies ran while one was open for 2% -> 2% of each run, Pallas kernels for 20% -> 14%
where the time goes in v2:
time: 127 us; the launch traced here: 126 us
  blocking collectives  52.4 us (41%)
  Pallas kernels  32.3 us (25%)
  waiting for transfers between devices  23.9 us (19%)
  starting transfers between devices  12.6 us (10%)
  local copies, waits for them, and re-layouts  4.87 us (4%)
    all_to_all x2, blocking collectives, swap(): return lax.all_to_all(array, axis, split_axis=0, concat_axis=0, tiled=True)  52.4 us
    all_to_all x2, waiting for transfers between devices, swap(): return lax.all_to_all(array, axis, split_axis=0, concat_axis=0, tiled=True)  23.9 us
    pallas_call x1, Pallas kernels, shards(): pl.pallas_call(ssm_kernel, out_shape=jax.ShapeDtypeStruct((BLOCKS, GROUP,...  17.4 us
    all_to_all x2, starting transfers between devices, swap(): return lax.all_to_all(array, axis, split_axis=0, concat_axis=0, tiled=True)  12.6 us
    pallas_call x1, Pallas kernels, shards(): pl.pallas_call(gate_kernel, out_shape=(jax.ShapeDtypeStruct((BLOCKS, GROU...  6.8 us
    pallas_call x1, Pallas kernels, shards(): pl.pallas_call(norm_kernel, out_shape=jax.ShapeDtypeStruct((BLOCKS, GROUP...  5.33 us
    unnamed x6, local copies, waits for them, and re-layouts  3.56 us
    pallas_call x1, Pallas kernels, shards(): pl.pallas_call(pack_kernel, out_shape=jax.ShapeDtypeStruct((BLOCKS, ROWS,...  2.75 us
  transfers between devices with their start and end apart: 2, of which 1 were waited for; matrix products, arithmetic and copies ran while one was open for 2% of the time, Pallas kernels for 14%

profile of v2, /device:TPU:2, one launch (start us, length us, event | category | flops | bytes accessed | tf_op | source)
XLA Modules:
  0.0 126.0 jit_solution(6272152385618151120)
XLA Ops:
  0.0 2.8 %pack.1 = bf16[16,264,256]{2,1,0:T(8,128)(2,1)} custom-call(bf16[1,128,4096]{2,1,0:T(8,128)(2,1)} %signal.1, bf16[1,128,128]{2,1,0:T(8,128)(2,1)} %bcf.1, bf16[1,128,128]{2,1,0:T(8,128)(2,1)} %bcb.1, bf16[1,128,128]{2,1,0:T(8,128)(2,1)} %step.1), custom_call_target="tpu_custom_call" | custom-call | bytes 4194304 | tf_op jit(solution)/shard_map/pack/pallas_call | solution.py:288
  2.8 5.9 %all-to-all-start = ((bf16[16,264,256]{2,1,0:T(8,128)(2,1)}), bf16[16,264,256]{2,1,0:T(8,128)(2,1)S(1)}, u32[]{:S(2)}, u32[]{:S(2)}) async-start(bf16[16,264,256]{2,1,0:T(8,128)(2,1)} %pack.1), calls=%async_computation | async-start | bytes 4325376 | tf_op jit(solution)/shard_map/all_to_all | solution.py:272
  8.6 1.6 %copy.11 = bf16[1,128,4096]{1,2,0:T(8,128)(2,1)S(1)} copy(bf16[1,128,4096]{2,1,0:T(8,128)(2,1)} %param.11) | data formatting | bytes 2097152 | tf_op args[1]
  10.2 1.3 %copy.12 = bf16[128,16,256]{2,0,1:T(8,128)(2,1)} copy(bf16[128,16,256]{0,2,1:T(8,128)(2,1)S(1)} %bitcast.3) | data formatting | bytes 2097152 | tf_op jit(solution)/shard_map/reshape;squeeze | solution.py:297
  11.5 23.9 %all-to-all-done.buf = bf16[16,264,256]{2,1,0:T(8,128)(2,1)S(1)} async-done(((bf16[16,264,256]{2,1,0:T(8,128)(2,1)}), bf16[16,264,256]{2,1,0:T(8,128)(2,1)S(1)}, u32[]{:S(2)}, u32[]{:S(2)}) %all-to-all-start) | async-done | bytes 2162720 | tf_op jit(solution)/shard_map/all_to_all | solution.py:272
  35.4 0.0 copy-start.1
  35.4 6.7 %all-to-all-start.1 = ((bf16[16,128,256]{2,1,0:T(8,128)(2,1)}), bf16[16,128,256]{2,1,0:T(8,128)(2,1)S(1)}, u32[]{:S(2)}, u32[]{:S(2)}) async-start(bf16[16,128,256]{2,1,0:T(8,128)(2,1)} %bitcast.1), calls=%async_computation.1 | async-start | bytes 2097152 | tf_op jit(solution)/shard_map/all_to_all | solution.py:272
  42.1 0.0 copy-done.1
  42.2 17.4 %ssm.1.y = f32[16,128,256]{2,1,0:T(8,128)} custom-call(bf16[16,264,256]{2,1,0:T(8,128)(2,1)} %copy-done.1, f32[2,4,4224]{2,1,0:T(4,128)} %cw.1, f32[2,4224]{1,0:T(2,128)} %cb.1, f32[2,64]{1,0:T(2,128)} %rate.1, f32[2,64]{1,0:T(2,128)} %skip.1), custom_call_target="tpu_custom_call" | custom-call | flops 20000000000 | bytes 8388608 | tf_op jit(solution)/shard_map/ssm/pallas_call | solution.py:299
  59.6 0.0 all-to-all-done.1.gate
  59.6 0.0 copy-start
  59.6 1.0 copy-done
  60.5 6.8 %gate.1 = (f32[16,128,256]{2,1,0:T(8,128)}, f32[16,16,128]{2,1,0:T(8,128)}) custom-call(f32[16,128,256]{2,1,0:T(8,128)} %ssm.1.y, bf16[16,128,256]{2,1,0:T(8,128)(2,1)} %copy-done), custom_call_target="tpu_custom_call" | custom-call | tf_op jit(solution)/shard_map/gate/pallas_call | solution.py:320
  67.3 10.7 %all_to_all.20.sums = f32[16,16,128]{2,1,0:T(8,128)} all-to-all(f32[16,16,128]{2,1,0:T(8,128)} %get-tuple-element.8), channel_id=1, replica_groups=mesh['tm'=16,'batch'=16] {'tm'}, dimensions={0} | all-to-all | bytes 262144 | tf_op jit(solution)/shard_map/all_to_all | solution.py:272
  78.0 5.3 %norm.1 = bf16[16,128,256]{2,1,0:T(8,128)(2,1)} custom-call(f32[16,128,256]{2,1,0:T(8,128)} %get-tuple-element.7.gated, f32[16,16,128]{2,1,0:T(8,128)} %all_to_all.20.sums, f32[1,4096]{1,0:T(1,128)} %bitcast.4), custom_call_target="tpu_custom_call" | custom-call | tf_op jit(solution)/shard_map/norm/pallas_call | solution.py:331
  83.4 41.7 %all_to_all.21 = bf16[16,128,256]{2,1,0:T(8,128)(2,1)S(1)} all-to-all(bf16[16,128,256]{2,1,0:T(8,128)(2,1)} %norm.1), channel_id=1, replica_groups=mesh['tm'=16,'batch'=16] {'batch'}, dimensions={0} | all-to-all | bytes 2097152 | tf_op jit(solution)/shard_map/all_to_all | solution.py:272
  125.1 1.0 copy.14
Async XLA Ops:
  2.8 32.7 %all-to-all-start = ((bf16[16,264,256]{2,1,0:T(8,128)(2,1)}), bf16[16,264,256]{2,1,0:T(8,128)(2,1)S(1)}, u32[]{:S(2)}, u32[]{:S(2)}) async-start(bf16[16,264,256]{2,1,0:T(8,128)(2,1)} %pack.1), calls=%async_computation | async-start | bytes 4325376 | tf_op jit(solution)/shard_map/all_to_all | solution.py:272
  35.4 6.7 %copy-start.1 = (bf16[16,264,256]{2,1,0:T(8,128)(2,1)}, bf16[16,264,256]{2,1,0:T(8,128)(2,1)S(1)}, u32[]{:S(2)}) copy-start(bf16[16,264,256]{2,1,0:T(8,128)(2,1)S(1)} %all-to-all-done.buf) | copy-start | bytes 6488068
  35.4 24.2 %all-to-all-start.1 = ((bf16[16,128,256]{2,1,0:T(8,128)(2,1)}), bf16[16,128,256]{2,1,0:T(8,128)(2,1)S(1)}, u32[]{:S(2)}, u32[]{:S(2)}) async-start(bf16[16,128,256]{2,1,0:T(8,128)(2,1)} %bitcast.1), calls=%async_computation.1 | async-start | bytes 2097152 | tf_op jit(solution)/shard_map/all_to_all | solution.py:272
  59.6 1.0 copy-start

commit v3 on v2

--- a/solution.py
+++ b/solution.py
@@ -15,24 +15,28 @@
 BLOCKS = 16
 OWN = 4
 WIDE = OWN * HEADDIM
-ROWS = 2 * GROUP + 8
+HALF = GROUP // 2
+ROWS = GROUP + HALF + 8
 EPSILON = 1e-05
-UNROLL_BC, UNROLL_X, UNROLL_Y = 2, 2, 2
+UNROLL_BC, UNROLL_X, UNROLL_Y = 8, 8, 4
 LOG2E = 1.4426950408889634
 VMEM = pl.BlockSpec(memory_space=pltpu.VMEM)
+LIMIT = pltpu.CompilerParams(vmem_limit_bytes=32 << 20)
 SMEM = pl.BlockSpec(memory_space=pltpu.SMEM)
 
 
-def pack_kernel(signal, bcf, bcb, step, out):
-    both = jnp.concatenate([bcf[0], bcb[0]], axis=1)
-    steps = step[0].astype(jnp.float32).T
-    for c in range(BLOCKS):
-        out[c, :GROUP] = signal[0, :, c * WIDE : (c + 1) * WIDE]
-        out[c, GROUP : 2 * GROUP] = both
+def pack_kernel(signal, bcf, bcb, step, out, turned):
+    turned[...] = step[0].astype(jnp.float32).T
+    at = pl.multiple_of(pl.program_id(0) * 4 * OWN, 4 * OWN)
+    forward, backward = turned[pl.ds(at, 4 * OWN)], turned[pl.ds(HEADS + at, 4 * OWN)]
+    for e in range(4):
+        out[e, :GROUP] = signal[0, :, e * WIDE : (e + 1) * WIDE]
+        bc = (bcf if e % 2 == 0 else bcb)[0]
+        out[e, GROUP : GROUP + HALF] = jnp.concatenate([bc[:HALF], bc[HALF:]], axis=1)
         mine = jnp.concatenate(
-            [steps[c * OWN : (c + 1) * OWN], steps[HEADS + c * OWN : HEADS + (c + 1) * OWN]], axis=0
+            [forward[e * OWN : (e + 1) * OWN], backward[e * OWN : (e + 1) * OWN]], axis=0
         )
-        out[c, 2 * GROUP :] = jnp.concatenate([mine, jnp.zeros_like(mine)], axis=1).astype(
+        out[e, GROUP + HALF :] = jnp.concatenate([mine, jnp.zeros_like(mine)], axis=1).astype(
             jnp.bfloat16
         )
 
@@ -51,13 +55,13 @@
 
 
 def ssm_kernel(
-    buf, cw, cb, rate, skip, y, raw, row_s, cum_s, dec_s, end_s, tot_s, fixed_s, x_s, c_s, bt_s, btb_s, st_s, carry_s
+    buf, other, cw, cb, rate, skip, y, ybuf, sent, raw, row_s, cum_s, dec_s, end_s, tot_s, fixed_s, x_s, c_s, bt_s, btb_s, st_s, carry_s
 ):
     f32, bf16 = jnp.float32, jnp.bfloat16
     tm = lax.axis_index("tm")
     n8 = BLOCKS * 8
 
-    raw_steps = buf[:, 2 * GROUP :, :GROUP].astype(f32).reshape(n8, GROUP)
+    raw_steps = buf[:, GROUP + HALF :, :GROUP].astype(f32).reshape(n8, GROUP)
     z = jnp.exp(-jnp.abs(raw_steps))
     u = 1.0 + z
     log1p = jnp.where(u == 1.0, z, jnp.log(u) * (z / jnp.where(u == 1.0, 1.0, u - 1.0)))
@@ -101,11 +105,16 @@
         raw[t, 0:8] = jnp.zeros((8, 128), f32)
         raw[t, 8 + BLOCKS * GROUP :] = jnp.zeros((8, 128), f32)
 
+    even = lax.rem(tm, 2) == 0
+
     def widen(i, _):
-        at = pl.ds(pl.multiple_of(8 + i * GROUP, 8), GROUP)
-        for t in range(4):
-            top = (t // 2) * GROUP
-            raw[t, at] = buf[i, top : top + GROUP, (t % 2) * 128 : (t % 2 + 1) * 128].astype(f32)
+        at = pl.multiple_of(8 + i * GROUP, 8)
+        for t in range(2):
+            raw[t, pl.ds(at, GROUP)] = buf[i, :GROUP, t * 128 : (t + 1) * 128].astype(f32)
+            near = buf[i, GROUP : GROUP + HALF, t * 128 : (t + 1) * 128].astype(f32)
+            far = other[i, :, t * 128 : (t + 1) * 128].astype(f32)
+            raw[2, pl.ds(at + t * HALF, HALF)] = jnp.where(even, near, far)
+            raw[3, pl.ds(at + t * HALF, HALF)] = jnp.where(even, far, near)
         return 0
 
     lax.fori_loop(0, BLOCKS, widen, 0)
@@ -223,49 +232,70 @@
                 preferred_element_type=f32,
             )
             local = jnp.where(low, local[:GROUP], local[GROUP:])
-            y[i, :, p * 128 : (p + 1) * 128] = local + wide[p]
+            ybuf[i, :, p * 128 : (p + 1) * 128] = local + wide[p]
+
+    def send(j):
+        at = pl.ds(j * UNROLL_Y, UNROLL_Y)
+        return pltpu.make_async_copy(ybuf.at[at], y.at[at], sent.at[j])
 
     def outputs(j, _):
+        @pl.when(j > 0)
+        def _():
+            send(j - 1).start()
+
         for e in range(UNROLL_Y):
             one_block(j * UNROLL_Y + e)
         return 0
 
-    lax.fori_loop(0, BLOCKS // UNROLL_Y, outputs, 0)
-
-
-def gate_kernel(y, gate, gated, sums):
-    def one(i, _):
-        g = y[i] * half_silu(gate[i].astype(jnp.float32) * 0.5)
-        gated[i] = g
-        total = lax.dot_general(
-            jnp.ones((8, WIDE), jnp.float32),
-            g * g,
-            (((1,), (1,)), ((), ())),
-            precision=lax.Precision.HIGHEST,
-            preferred_element_type=jnp.float32,
-        )
-        sums[:, pl.ds(i, 1), :] = jnp.broadcast_to(total[:1][None], (BLOCKS, 1, GROUP))
+    count = BLOCKS // UNROLL_Y
+    lax.fori_loop(0, count, outputs, 0)
+    send(count - 1).start()
+    for j in range(count):
+        send(j).wait()
+
+
+def gate_kernel(y, gate, gated, sums, ybuf, came):
+    f32, bf16 = jnp.float32, jnp.bfloat16
+
+    def fetch(j):
+        at = pl.ds(j * 4, 4)
+        return pltpu.make_async_copy(y.at[at], ybuf.at[at], came.at[j])
+
+    for j in range(BLOCKS // 4):
+        fetch(j).start()
+
+    def four(j, _):
+        fetch(j).wait()
+        for e in range(4):
+            i = j * 4 + e
+            g = ybuf[i] * half_silu(gate[i].astype(f32) * 0.5)
+            gated[i] = g
+            square = g * g
+            square = square[:, :128] + square[:, 128:]
+            high = square.astype(bf16)
+            parts = jnp.concatenate([high, (square - high.astype(f32)).astype(bf16)], axis=1)
+            total = lax.dot_general(
+                jnp.ones((8, WIDE), bf16), parts, (((1,), (1,)), ((), ())), preferred_element_type=f32
+            )
+            sums[:, pl.ds(i, 1), :] = jnp.broadcast_to(total[:1][None], (BLOCKS, 1, GROUP))
         return 0
 
-    lax.fori_loop(0, BLOCKS, one, 0)
-
-
-def norm_kernel(gated, sums, gain, out, inv_s):
+    lax.fori_loop(0, BLOCKS // 4, four, 0)
+
+
+def norm_kernel(gated, sums, gain, out):
     gains = gain[0:1, pl.ds(pl.multiple_of(lax.axis_index("tm") * WIDE, WIDE), WIDE)]
     total = sums[0]
     for k in range(1, BLOCKS):
         total = total + sums[k]
     inv = lax.rsqrt(total * (1.0 / INNER) + EPSILON)
-    inv_s[...] = jnp.concatenate(
-        [inv, jnp.zeros((GROUP - BLOCKS, GROUP), jnp.float32)], axis=0
-    ).T
-
-    def one(i, _):
-        scale = pltpu.roll(inv_s[...], (GROUP - i) % GROUP, 1)[:, :1]
-        out[i] = (gated[i] * scale * gains).astype(jnp.bfloat16)
-        return 0
-
-    lax.fori_loop(0, BLOCKS, one, 0)
+    columns = jnp.concatenate([inv, jnp.zeros((GROUP - BLOCKS, GROUP), jnp.float32)], axis=0).T
+    for i in range(BLOCKS):
+        out[i] = (gated[i] * columns[:, i : i + 1] * gains).astype(jnp.bfloat16)
+
+
+def local(array):
+    return pltpu.with_memory_space_constraint(array, pltpu.VMEM)
 
 
 def swap(array, axis):
@@ -287,21 +317,32 @@
     f32, bf16 = jnp.float32, jnp.bfloat16
     packed = pl.pallas_call(
         pack_kernel,
+        grid=(4,),
         out_shape=jax.ShapeDtypeStruct((BLOCKS, ROWS, WIDE), bf16),
-        in_specs=[VMEM] * 4,
-        out_specs=VMEM,
+        in_specs=[
+            pl.BlockSpec((1, GROUP, 4 * WIDE), lambda i: (0, 0, i)),
+            *[pl.BlockSpec((1, GROUP, 128), lambda i: (0, 0, 0))] * 3,
+        ],
+        out_specs=pl.BlockSpec((4, ROWS, WIDE), lambda i: (i, 0, 0)),
+        scratch_shapes=[pltpu.VMEM((GROUP, 128), f32)],
         name="pack",
-        cost_estimate=pl.CostEstimate(flops=0, bytes_accessed=4 << 20, transcendentals=0),
+        cost_estimate=pl.CostEstimate(flops=0, bytes_accessed=3 << 20, transcendentals=0),
     )(signal, bc_forward, bc_backward, step_raw)
-    got = swap(packed, "tm")
     gates = gate_input[0].reshape(GROUP, BLOCKS, WIDE).transpose(1, 0, 2)
+    got, gates = lax.optimization_barrier((swap(packed, "tm"), gates))
+    other = lax.ppermute(
+        got[:, GROUP : GROUP + HALF], "tm", [(i, i ^ 1) for i in range(BLOCKS)]
+    )
     gates = swap(gates, "tm")
     y = pl.pallas_call(
         ssm_kernel,
-        out_shape=jax.ShapeDtypeStruct((BLOCKS, GROUP, WIDE), f32),
-        in_specs=[VMEM, VMEM, VMEM, SMEM, SMEM],
-        out_specs=VMEM,
+        out_shape=pltpu.HBM((BLOCKS, GROUP, WIDE), f32),
+        compiler_params=LIMIT,
+        in_specs=[VMEM, VMEM, VMEM, VMEM, SMEM, SMEM],
+        out_specs=pl.BlockSpec(memory_space=pl.ANY),
         scratch_shapes=[
+            pltpu.VMEM((BLOCKS, GROUP, WIDE), f32),
+            pltpu.SemaphoreType.DMA((BLOCKS // UNROLL_Y,)),
             pltpu.VMEM((4, BLOCKS * GROUP + 16, 128), f32),
             *[pltpu.VMEM((BLOCKS * 8, GROUP), f32)] * 5,
             pltpu.VMEM((12, 96, 128), bf16),
@@ -316,26 +357,31 @@
         cost_estimate=pl.CostEstimate(
             flops=20_000_000_000, bytes_accessed=8 << 20, transcendentals=4_000_000
         ),
-    )(got, conv_weight, conv_bias, decay_rate, skip_gain)
+    )(local(got), local(other), conv_weight, conv_bias, decay_rate, skip_gain)
     gated, sums = pl.pallas_call(
         gate_kernel,
         out_shape=(
-            jax.ShapeDtypeStruct((BLOCKS, GROUP, WIDE), f32),
-            jax.ShapeDtypeStruct((BLOCKS, BLOCKS, GROUP), f32),
+            pltpu.VMEM((BLOCKS, GROUP, WIDE), f32),
+            pltpu.VMEM((BLOCKS, BLOCKS, GROUP), f32),
         ),
-        in_specs=[VMEM] * 2,
+        compiler_params=LIMIT,
+        in_specs=[pl.BlockSpec(memory_space=pl.ANY), VMEM],
         out_specs=(VMEM, VMEM),
+        scratch_shapes=[
+            pltpu.VMEM((BLOCKS, GROUP, WIDE), f32),
+            pltpu.SemaphoreType.DMA((BLOCKS // 4,)),
+        ],
         name="gate",
-    )(y, gates)
+    )(pltpu.with_memory_space_constraint(y, pltpu.HBM), local(gates))
     sums = swap(sums, "tm")
     normed = pl.pallas_call(
         norm_kernel,
-        out_shape=jax.ShapeDtypeStruct((BLOCKS, GROUP, WIDE), bf16),
+        out_shape=pltpu.VMEM((BLOCKS, GROUP, WIDE), bf16),
+        compiler_params=LIMIT,
         in_specs=[VMEM] * 3,
         out_specs=VMEM,
-        scratch_shapes=[pltpu.VMEM((GROUP, GROUP), f32)],
         name="norm",
-    )(gated, sums, norm_gain[None])
+    )(local(gated), local(sums), norm_gain[None])
     return swap(normed, "batch")
 
 

time: 127 us -> 107 us (0.84)
  Pallas kernels: 32.3 us -> 19 us
  waiting for transfers between devices: 23.9 us -> 19.7 us
    pallas_call x4, Pallas kernels: 32.3 us -> 19 us  [the longest x1 12.6 us: shards(): pl.pallas_call(ssm_kernel, out_shape=pltpu.HBM((BLOCKS, GROUP, WIDE), f32...]
    all_to_all x2, waiting for transfers between devices: 23.9 us -> 19.6 us  [swap(): return lax.all_to_all(array, axis, split_axis=0, concat_axis=0, tiled=True)]
    unnamed x6 -> x12, local copies, waits for them, and re-layouts: 3.56 us -> 2.6 us
  transfers between devices with their start and end apart: 2 -> 3, of which waited for: 1 -> 2; matrix products, arithmetic and copies ran while one was open for 2% -> 3% of each run, Pallas kernels for 14% -> 12%
where the time goes in v3:
time: 107 us
  blocking collectives  51.4 us (48%)
  waiting for transfers between devices  19.7 us (18%)
  Pallas kernels  19 us (18%)
  starting transfers between devices  12.1 us (11%)
  local copies, waits for them, and re-layouts  4.76 us (4%)
    all_to_all x2, blocking collectives, swap(): return lax.all_to_all(array, axis, split_axis=0, concat_axis=0, tiled=True)  51.4 us
    all_to_all x2, waiting for transfers between devices, swap(): return lax.all_to_all(array, axis, split_axis=0, concat_axis=0, tiled=True)  19.6 us
    pallas_call x1, Pallas kernels, shards(): pl.pallas_call(ssm_kernel, out_shape=pltpu.HBM((BLOCKS, GROUP, WIDE), f32...  12.6 us
    all_to_all x2, starting transfers between devices, swap(): return lax.all_to_all(array, axis, split_axis=0, concat_axis=0, tiled=True)  12.1 us
    pallas_call x1, Pallas kernels, shards(): pl.pallas_call(pack_kernel, grid=(4,), out_shape=jax.ShapeDtypeStruct((BL...  3.67 us
    unnamed x12, local copies, waits for them, and re-layouts  2.6 us
    pallas_call x1, Pallas kernels, shards(): pl.pallas_call(gate_kernel, out_shape=(pltpu.VMEM((BLOCKS, GROUP, WIDE),...  2.21 us
  transfers between devices with their start and end apart: 3, of which 2 were waited for; matrix products, arithmetic and copies ran while one was open for 3% of the time, Pallas kernels for 12%

profile of v3, /device:TPU:2, one launch (start us, length us, event | category | flops | bytes accessed | tf_op | source)
XLA Modules:
  0.0 107.0 jit_solution(12903056677596938621)
XLA Ops:
  0.0 3.7 %pack.1 = bf16[16,200,256]{2,1,0:T(8,128)(2,1)} custom-call(bf16[1,128,4096]{2,1,0:T(8,128)(2,1)} %signal.1, bf16[1,128,128]{2,1,0:T(8,128)(2,1)} %bcf.1, bf16[1,128,128]{2,1,0:T(8,128)(2,1)} %bcb.1, bf16[1,128,128]{2,1,0:T(8,128)(2,1)} %step.1), custom_call_target="tpu_custom_call" | custom-call | bytes 3145728 | tf_op jit(solution)/shard_map/pack/pallas_call | solution.py:318
  3.7 5.9 %all-to-all-start = ((bf16[16,200,256]{2,1,0:T(8,128)(2,1)}), bf16[16,200,256]{2,1,0:T(8,128)(2,1)S(1)}, u32[]{:S(2)}, u32[]{:S(2)}) async-start(bf16[16,200,256]{2,1,0:T(8,128)(2,1)} %pack.1), calls=%async_computation | async-start | bytes 3276800 | tf_op jit(solution)/shard_map/all_to_all | solution.py:302
  9.5 1.6 %copy.11 = bf16[1,128,4096]{1,2,0:T(8,128)(2,1)S(1)} copy(bf16[1,128,4096]{2,1,0:T(8,128)(2,1)} %param.11) | data formatting | bytes 2097152 | tf_op args[1]
  11.2 1.3 %copy.12 = bf16[128,16,256]{2,0,1:T(8,128)(2,1)} copy(bf16[128,16,256]{0,2,1:T(8,128)(2,1)S(1)} %bitcast.5) | data formatting | bytes 2097152 | tf_op jit(solution)/shard_map/reshape;squeeze | solution.py:331
  12.5 0.0 copy-start.1
  12.5 0.0 copy-start.2
  12.5 0.0 copy-start.3
  12.5 0.0 copy-start.4
  12.5 18.0 %all-to-all-done.buf = bf16[16,200,256]{2,1,0:T(8,128)(2,1)S(1)} async-done(((bf16[16,200,256]{2,1,0:T(8,128)(2,1)}), bf16[16,200,256]{2,1,0:T(8,128)(2,1)S(1)}, u32[]{:S(2)}, u32[]{:S(2)}) %all-to-all-start) | async-done | bytes 1638432 | tf_op jit(solution)/shard_map/all_to_all | solution.py:302
  30.5 0.8 slice.3
  31.3 0.0 collective-permute-start
  31.3 6.3 %all-to-all-start.1 = ((bf16[16,128,256]{2,1,0:T(8,128)(2,1)}), bf16[16,128,256]{2,1,0:T(8,128)(2,1)S(1)}, u32[]{:S(2)}, u32[]{:S(2)}) async-start(bf16[16,128,256]{2,1,0:T(8,128)(2,1)} %bitcast.4), calls=%async_computation.1 | async-start | bytes 2097152 | tf_op jit(solution)/shard_map/all_to_all | solution.py:302
  37.6 0.0 collective-permute-done.other
  37.6 0.0 copy-done.1
  37.6 0.0 copy-done.2
  37.6 0.0 copy-done.3
  37.6 0.0 copy-done.4
  37.6 12.6 %ssm.1.y = f32[16,128,256]{2,1,0:T(8,128)} custom-call(bf16[16,200,256]{2,1,0:T(8,128)(2,1)S(1)} %all-to-all-done.buf, bf16[16,64,256]{2,1,0:T(8,128)(2,1)S(1)} %collective-permute-done.other, f32[2,4,4224]{2,1,0:T(4,128)S(1)} %copy-done.1, f32[2,4224]{1,0:T(2,128)S(1)} %copy-done.2, f32[2,64]{1,0:T(2,128)S(1)} %copy-done.3, f32[2,64]{1,0:T(2,128)S(1)} %copy-done.4), custom_call_target="tpu_custom_call" | custom-call | flops 20000000000 | bytes 8388608 | tf_op jit(solution)/shard_map/ssm/pallas_call | solution.py:337
  50.3 0.0 copy-start
  50.3 1.6 %all-to-all-done.1.gate = bf16[16,128,256]{2,1,0:T(8,128)(2,1)S(1)} async-done(((bf16[16,128,256]{2,1,0:T(8,128)(2,1)}), bf16[16,128,256]{2,1,0:T(8,128)(2,1)S(1)}, u32[]{:S(2)}, u32[]{:S(2)}) %all-to-all-start.1) | async-done | bytes 1048608 | tf_op jit(solution)/shard_map/all_to_all | solution.py:302
  51.9 2.2 %gate.1 = (f32[16,128,256]{2,1,0:T(8,128)S(1)}, f32[16,16,128]{2,1,0:T(8,128)S(1)}) custom-call(f32[16,128,256]{2,1,0:T(8,128)} %ssm.1.y, bf16[16,128,256]{2,1,0:T(8,128)(2,1)S(1)} %all-to-all-done.1.gate), custom_call_target="tpu_custom_call" | custom-call | tf_op jit(solution)/shard_map/gate/pallas_call | solution.py:361
  54.2 9.9 %all_to_all.20.sums = f32[16,16,128]{2,1,0:T(8,128)S(1)} all-to-all(f32[16,16,128]{2,1,0:T(8,128)S(1)} %get-tuple-element.12), channel_id=1, replica_groups=mesh['tm'=16,'batch'=16] {'tm'}, dimensions={0} | all-to-all | bytes 262144 | tf_op jit(solution)/shard_map/all_to_all | solution.py:302
  64.1 0.0 copy-done
  64.1 0.5 norm.1
  64.6 41.5 %all_to_all.21 = bf16[16,128,256]{2,1,0:T(8,128)(2,1)S(1)} all-to-all(bf16[16,128,256]{2,1,0:T(8,128)(2,1)S(1)} %norm.1), channel_id=1, replica_groups=mesh['tm'=16,'batch'=16] {'batch'}, dimensions={0} | all-to-all | bytes 2097152 | tf_op jit(solution)/shard_map/all_to_all | solution.py:302
  106.1 1.0 copy.14
Async XLA Ops:
  3.7 26.8 %all-to-all-start = ((bf16[16,200,256]{2,1,0:T(8,128)(2,1)}), bf16[16,200,256]{2,1,0:T(8,128)(2,1)S(1)}, u32[]{:S(2)}, u32[]{:S(2)}) async-start(bf16[16,200,256]{2,1,0:T(8,128)(2,1)} %pack.1), calls=%async_computation | async-start | bytes 3276800 | tf_op jit(solution)/shard_map/all_to_all | solution.py:302
  12.5 25.1 %copy-start.1 = (f32[2,4,4224]{2,1,0:T(4,128)S(1)}, f32[2,4,4224]{2,1,0:T(4,128)}, u32[]{:S(2)}) copy-start(f32[2,4,4224]{2,1,0:T(4,128)} %cw.1) | copy-start | bytes 405508
  12.5 25.2 %copy-start.2 = (f32[2,4224]{1,0:T(2,128)S(1)}, f32[2,4224]{1,0:T(2,128)}, u32[]{:S(2)}) copy-start(f32[2,4224]{1,0:T(2,128)} %cb.1) | copy-start | bytes 101380
  12.5 25.2 %copy-start.3 = (f32[2,64]{1,0:T(2,128)S(1)}, f32[2,64]{1,0:T(2,128)}, u32[]{:S(2)}) copy-start(f32[2,64]{1,0:T(2,128)} %rate.1) | copy-start | bytes 1540
  12.5 25.2 %copy-start.4 = (f32[2,64]{1,0:T(2,128)S(1)}, f32[2,64]{1,0:T(2,128)}, u32[]{:S(2)}) copy-start(f32[2,64]{1,0:T(2,128)} %skip.1) | copy-start | bytes 1540
  31.3 6.3 %collective-permute-start = (bf16[16,64,256]{2,1,0:T(8,128)(2,1)}, bf16[16,64,256]{2,1,0:T(8,128)(2,1)S(1)}, u32[]{:S(2)}, u32[]{:S(2)}) collective-permute-start(bf16[16,64,256]{2,1,0:T(8,128)(2,1)} %slice.3), channel_id=1, source_target_pairs={{0,16},{16,0},{32,48},{48,32},{64,80},{80,64},{96,112},{112,96},{1... | collective-permute-start | bytes 1572872 | tf_op jit(solution)/shard_map/ppermute | solution.py:333
  31.3 20.6 %all-to-all-start.1 = ((bf16[16,128,256]{2,1,0:T(8,128)(2,1)}), bf16[16,128,256]{2,1,0:T(8,128)(2,1)S(1)}, u32[]{:S(2)}, u32[]{:S(2)}) async-start(bf16[16,128,256]{2,1,0:T(8,128)(2,1)} %bitcast.4), calls=%async_computation.1 | async-start | bytes 2097152 | tf_op jit(solution)/shard_map/all_to_all | solution.py:302
  50.3 13.8 %copy-start = (f32[4096]{0:T(1024)S(1)}, f32[4096]{0:T(1024)}, u32[]{:S(2)}) copy-start(f32[4096]{0:T(1024)} %param.19) | copy-start | bytes 49156
